TPU v7x, 32 devices: a whole 2x2x4 slice. The times are simulated.
32 devices in a mesh: dp: 8 (over y, x, core), tensor: 4 (over z).
Axes of the slice: x: 2, y: 2, z: 4, core: 2. Of those that a mesh axis runs over, the one named last changes fastest.
Arguments:
- inputs: bfloat16 [16, 1024, 1024], P('dp', 'tensor'), may hold values from -6 to 6
- lengths: int32 [16], P('dp'), may hold values from 256 to 1024, as said below
- w_query: bfloat16 [1024, 1024], P('dp', 'tensor'), may hold values from -0.1875 to 0.1875
- w_key: bfloat16 [1024, 1024], P('dp', 'tensor'), may hold values from -0.1875 to 0.1875
- w_value: bfloat16 [1024, 1024], P('dp', 'tensor'), may hold values from -0.1875 to 0.1875
- b_query: bfloat16 [1024], P('tensor'), may hold values from -3 to 3
- b_value: bfloat16 [1024], P('tensor'), may hold values from -0.29882812 to 0.29882812
- w_out: bfloat16 [1024, 1024], P('tensor', 'dp'), may hold values from -1.5 to 1.5
- b_out: bfloat16 [1024], replicated, may hold values from -3 to 3
- gain_one: bfloat16 [1024], replicated, may hold values from 0.099609375 to 1.8984375
- shift_one: bfloat16 [1024], replicated, may hold values from -3 to 3
- w_in: bfloat16 [1024, 4096], P('dp', 'tensor'), may hold values from -0.1875 to 0.1875
- b_in: bfloat16 [4096], P('tensor'), may hold values from -3 to 3
- w_back: bfloat16 [4096, 1024], P('tensor', 'dp'), may hold values from -0.09375 to 0.09375
- b_back: bfloat16 [1024], replicated, may hold values from -3 to 3
- gain_two: bfloat16 [1024], replicated, may hold values from 0.099609375 to 1.8984375
- shift_two: bfloat16 [1024], replicated, may hold values from -3 to 3
- cotangent: bfloat16 [16, 1024, 1024], P('dp', 'tensor'), may hold values from -6 to 6
Outputs:
- layer_out: bfloat16 [16, 1024, 1024], P('dp', 'tensor')
- grad_inputs: float32 [16, 1024, 1024], P('dp', 'tensor')
- grad_w_query: float32 [1024, 1024], P('dp', 'tensor')
- grad_w_key: float32 [1024, 1024], P('dp', 'tensor')
- grad_w_value: float32 [1024, 1024], P('dp', 'tensor')
- grad_b_query: float32 [1024], P('tensor')
- grad_b_value: float32 [1024], P('tensor')
- grad_w_out: float32 [1024, 1024], P('tensor', 'dp')
- grad_b_out: float32 [1024], replicated
- grad_gain_one: float32 [1024], replicated
- grad_shift_one: float32 [1024], replicated
- grad_w_in: float32 [1024, 4096], P('dp', 'tensor')
- grad_b_in: float32 [4096], P('tensor')
- grad_w_back: float32 [4096, 1024], P('tensor', 'dp')
- grad_b_back: float32 [1024], replicated
- grad_gain_two: float32 [1024], replicated
- grad_shift_two: float32 [1024], replicated
Inputs may be any that keep to these rules, and one draw needn't show every extreme that they name: The first lengths[s] slots of sequence s are real tokens; one sequence has 1024 and another 1024 // 4.
All inputs are finite; a program needn't handle non-finite values.
Results may differ from a plain program's by a relative error of at most 0.015.
The roundings to bfloat16 on the way count: a program that leaves them out, or rounds other values in their place, can miss the bound.
Values may be sent and summed in bfloat16 or wider, within the bound.
A program may use at most 192 MiB of HBM per device.

v0:
```python
from functools import partial
import jax
import jax.numpy as jnp
from jax import lax
from jax.sharding import PartitionSpec as P

HD = 64
EPSILON = 1e-05
NEGATIVE = -1e30


def norm_rows(values, norm_gain, norm_shift):
    average = jnp.mean(values, axis=-1, keepdims=True)
    centered = values - average
    variance = jnp.mean(centered * centered, axis=-1, keepdims=True)
    return centered * lax.rsqrt(variance + EPSILON) * norm_gain + norm_shift


def gelu_exact(values):
    return jax.nn.gelu(values, approximate=False)


def contract_rows(left_side, right_side):
    return lax.dot_general(
        left_side, right_side, (((0,), (0,)), ((), ())), preferred_element_type=jnp.float32
    )


def contract_cols(left_side, right_side):
    return lax.dot_general(
        left_side, right_side, (((1,), (1,)), ((), ())), preferred_element_type=jnp.float32
    )


def attend_forward(query_rows, key_rows, value_rows, key_valid):
    scores = jnp.einsum("qhd,khd->hqk", query_rows, key_rows, preferred_element_type=jnp.float32)
    scores = jnp.where(key_valid[None, None, :], scores, NEGATIVE)
    largest = jnp.max(scores, axis=-1, keepdims=True)
    weights = jnp.exp(scores - largest)
    row_total = jnp.sum(weights, axis=-1, keepdims=True)
    chances = (weights / row_total).astype(jnp.bfloat16)
    context = jnp.einsum("hqk,khd->qhd", chances, value_rows, preferred_element_type=jnp.float32)
    return (context, largest[:, :, 0] + jnp.log(row_total[:, :, 0]))


def attend_backward(log_total, grad_context, query_rows, key_rows, value_rows, key_valid):
    scores = jnp.einsum("qhd,khd->hqk", query_rows, key_rows, preferred_element_type=jnp.float32)
    scores = jnp.where(key_valid[None, None, :], scores, NEGATIVE)
    chances = jnp.exp(scores - log_total[:, :, None])
    grad_values = jnp.einsum(
        "hqk,qhd->khd",
        chances.astype(jnp.bfloat16),
        grad_context,
        preferred_element_type=jnp.float32,
    )
    grad_chances = jnp.einsum(
        "qhd,khd->hqk", grad_context, value_rows, preferred_element_type=jnp.float32
    )
    inner = jnp.sum(grad_chances * chances, axis=-1, keepdims=True)
    grad_scores = (chances * (grad_chances - inner)).astype(jnp.bfloat16)
    grad_queries = jnp.einsum(
        "hqk,khd->qhd", grad_scores, key_rows, preferred_element_type=jnp.float32
    )
    grad_keys = jnp.einsum(
        "hqk,qhd->khd", grad_scores, query_rows, preferred_element_type=jnp.float32
    )
    return (grad_queries, grad_keys, grad_values)


def fetch_weights(w_query, w_key, w_value, w_in, w_out, w_back):
    gathered_rows = (
        lax.all_gather(w_query, "dp", axis=0, tiled=True),
        lax.all_gather(w_key, "dp", axis=0, tiled=True),
        lax.all_gather(w_value, "dp", axis=0, tiled=True),
        lax.all_gather(w_in, "dp", axis=0, tiled=True),
    )
    gathered_columns = (
        lax.all_gather(w_out, "dp", axis=1, tiled=True),
        lax.all_gather(w_back, "dp", axis=1, tiled=True),
    )
    joined = jnp.concatenate([gathered_rows[0], gathered_rows[1], gathered_rows[2]], axis=1)
    return (joined, gathered_rows[3], gathered_columns[0], gathered_columns[1])


def on_device(
    inputs,
    lengths,
    w_query,
    w_key,
    w_value,
    b_query,
    b_value,
    w_out,
    b_out,
    gain_one,
    shift_one,
    w_in,
    b_in,
    w_back,
    b_back,
    gain_two,
    shift_two,
    cotangent,
):
    f32 = jnp.float32
    bf16 = jnp.bfloat16
    tensor_size = lax.axis_size("tensor")
    rows_here = inputs.shape[1]
    slots = rows_here * tensor_size
    local_width = w_query.shape[1]
    local_hidden = w_in.shape[1]
    local_heads = local_width // HD
    query_scale = HD ** (-0.5)
    block_rows = min(512, slots)
    row_place = lax.axis_index("tensor") * rows_here + jnp.arange(rows_here)
    query_bias = b_query.astype(f32)
    value_bias = b_value.astype(f32)
    out_bias = b_out.astype(f32)
    in_bias = b_in.astype(f32)
    back_bias = b_back.astype(f32)
    gain_first = gain_one.astype(f32)
    shift_first = shift_one.astype(f32)
    gain_second = gain_two.astype(f32)
    shift_second = shift_two.astype(f32)

    def one_batch(totals_now, batch_item):
        own_rows, length, grad_own = batch_item
        joined, matrix_in, matrix_out, matrix_back = fetch_weights(
            w_query, w_key, w_value, w_in, w_out, w_back
        )
        row_valid = row_place < length
        key_valid = jnp.arange(slots) < length
        full_in = lax.all_gather(own_rows, "tensor", axis=0, tiled=True)
        projected = jnp.dot(full_in, joined, preferred_element_type=f32)
        query_all = ((projected[:, :local_width] + query_bias) * query_scale).astype(bf16)
        key_all = projected[:, local_width : 2 * local_width].astype(bf16)
        value_all = (projected[:, 2 * local_width :] + value_bias).astype(bf16)
        query_heads = query_all.reshape(slots, local_heads, HD)
        key_heads = key_all.reshape(slots, local_heads, HD)
        value_heads = value_all.reshape(slots, local_heads, HD)
        context_blocks = []
        log_blocks = []
        for row_start in range(0, slots, block_rows):
            query_block = query_heads[row_start : row_start + block_rows]
            produced = attend_forward(query_block, key_heads, value_heads, key_valid)
            context_blocks.append(produced[0])
            log_blocks.append(produced[1])
        context_low = (
            jnp.concatenate(context_blocks, axis=0).reshape(slots, local_width).astype(bf16)
        )
        log_total = jnp.concatenate(log_blocks, axis=1)
        attended = lax.psum_scatter(
            jnp.dot(context_low, matrix_out, preferred_element_type=f32),
            "tensor",
            scatter_dimension=0,
            tiled=True,
        )
        first_sum = own_rows.astype(f32) + attended + out_bias
        first_norm, first_back = jax.vjp(norm_rows, first_sum, gain_first, shift_first)
        first_low = first_norm.astype(bf16)
        full_first = lax.all_gather(first_low, "tensor", axis=0, tiled=True)
        pre_act = jnp.dot(full_first, matrix_in, preferred_element_type=f32) + in_bias
        activated, gelu_back = jax.vjp(gelu_exact, pre_act)
        hidden_low = activated.astype(bf16)
        mixed_rows = lax.psum_scatter(
            jnp.dot(hidden_low, matrix_back, preferred_element_type=f32),
            "tensor",
            scatter_dimension=0,
            tiled=True,
        )
        second_sum = first_norm + mixed_rows + back_bias
        second, second_back = jax.vjp(norm_rows, second_sum, gain_second, shift_second)
        layer_rows = jnp.where(row_valid[:, None], second, 0.0).astype(bf16)
        joined, matrix_in, matrix_out, matrix_back = fetch_weights(
            w_query, w_key, w_value, w_in, w_out, w_back
        )
        grad_second = jnp.where(row_valid[:, None], grad_own.astype(f32), 0.0)
        grad_mixed, grad_gain_b, grad_shift_b = second_back(grad_second)
        full_grad_mixed = lax.all_gather(grad_mixed.astype(bf16), "tensor", axis=0, tiled=True)
        grad_activated = contract_cols(full_grad_mixed, matrix_back)
        grad_back_w = contract_rows(hidden_low, full_grad_mixed)
        (grad_pre,) = gelu_back(grad_activated)
        grad_pre_low = grad_pre.astype(bf16)
        grad_in_bias = jnp.sum(grad_pre_low.astype(f32), axis=0)
        grad_in_w = contract_rows(full_first, grad_pre_low)
        grad_first_mix = lax.psum_scatter(
            contract_cols(grad_pre_low, matrix_in), "tensor", scatter_dimension=0, tiled=True
        )
        grad_first = grad_mixed + grad_first_mix
        grad_att, grad_gain_a, grad_shift_a = first_back(grad_first)
        full_grad_att = lax.all_gather(grad_att.astype(bf16), "tensor", axis=0, tiled=True)
        grad_context = contract_cols(full_grad_att, matrix_out).astype(bf16)
        grad_out_w = contract_rows(context_low, full_grad_att)
        grad_context_heads = grad_context.reshape(slots, local_heads, HD)
        query_grad_blocks = []
        key_grad_sum = jnp.zeros((slots, local_heads, HD), f32)
        value_grad_sum = jnp.zeros((slots, local_heads, HD), f32)
        for row_start in range(0, slots, block_rows):
            query_block = query_heads[row_start : row_start + block_rows]
            block_fn = partial(
                attend_backward,
                log_total[:, row_start : row_start + block_rows],
                grad_context_heads[row_start : row_start + block_rows],
            )
            produced = block_fn(query_block, key_heads, value_heads, key_valid)
            query_grad_blocks.append(produced[0])
            key_grad_sum = key_grad_sum + produced[1]
            value_grad_sum = value_grad_sum + produced[2]
        grad_query_low = (
            jnp.concatenate(query_grad_blocks, axis=0).reshape(slots, local_width).astype(bf16)
        )
        grad_key_low = key_grad_sum.reshape(slots, local_width).astype(bf16)
        grad_value_low = value_grad_sum.reshape(slots, local_width).astype(bf16)
        grad_projected = jnp.concatenate(
            [grad_query_low * query_scale, grad_key_low, grad_value_low], axis=1
        )
        grad_joined_w = contract_rows(full_in, grad_projected)
        grad_query_bias = jnp.sum(grad_projected[:, :local_width].astype(f32), axis=0)
        grad_value_bias = jnp.sum(grad_value_low.astype(f32), axis=0)
        grad_input_mix = lax.psum_scatter(
            contract_cols(grad_projected, joined).astype(jnp.bfloat16),
            "tensor",
            scatter_dimension=0,
            tiled=True,
        ).astype(jnp.float32)
        grad_rows = grad_att + grad_input_mix
        increments = (
            grad_joined_w,
            grad_out_w,
            grad_in_w,
            grad_back_w,
            grad_query_bias,
            grad_value_bias,
            grad_in_bias,
            jnp.sum(grad_att, axis=0),
            grad_gain_a,
            grad_shift_a,
            jnp.sum(grad_mixed, axis=0),
            grad_gain_b,
            grad_shift_b,
        )
        totals_next = jax.tree.map(jnp.add, totals_now, increments)
        return (totals_next, (layer_rows, grad_rows))

    model_width = w_out.shape[1] * lax.axis_size("dp")
    starting = (
        jnp.zeros((model_width, 3 * local_width), f32),
        jnp.zeros((local_width, model_width), f32),
        jnp.zeros((model_width, local_hidden), f32),
        jnp.zeros((local_hidden, model_width), f32),
        jnp.zeros((local_width,), f32),
        jnp.zeros((local_width,), f32),
        jnp.zeros((local_hidden,), f32),
        jnp.zeros((model_width,), f32),
        jnp.zeros((model_width,), f32),
        jnp.zeros((model_width,), f32),
        jnp.zeros((model_width,), f32),
        jnp.zeros((model_width,), f32),
        jnp.zeros((model_width,), f32),
    )
    totals, stacked = lax.scan(one_batch, starting, (inputs, lengths, cotangent))
    layer_out, grad_inputs = stacked
    grad_joined_w = totals[0]
    reduced_rows = (
        lax.psum_scatter(grad_joined_w[:, :local_width], "dp", scatter_dimension=0, tiled=True),
        lax.psum_scatter(
            grad_joined_w[:, local_width : 2 * local_width], "dp", scatter_dimension=0, tiled=True
        ),
        lax.psum_scatter(
            grad_joined_w[:, 2 * local_width :], "dp", scatter_dimension=0, tiled=True
        ),
        lax.psum_scatter(totals[2], "dp", scatter_dimension=0, tiled=True),
    )
    reduced_columns = (
        lax.psum_scatter(totals[1], "dp", scatter_dimension=1, tiled=True),
        lax.psum_scatter(totals[3], "dp", scatter_dimension=1, tiled=True),
    )
    bias_sums = lax.psum((totals[4], totals[5], totals[6]), "dp")
    norm_sums = lax.psum(
        (totals[7], totals[8], totals[9], totals[10], totals[11], totals[12]), ("dp", "tensor")
    )
    return (
        layer_out,
        grad_inputs,
        reduced_rows[0],
        reduced_rows[1],
        reduced_rows[2],
        bias_sums[0],
        bias_sums[1],
        reduced_columns[0],
        norm_sums[0],
        norm_sums[1],
        norm_sums[2],
        reduced_rows[3],
        bias_sums[2],
        reduced_columns[1],
        norm_sums[3],
        norm_sums[4],
        norm_sums[5],
    )


def solution(mesh):
    return jax.shard_map(
        on_device,
        mesh=mesh,
        in_specs=(
            P("dp", "tensor", None),
            P("dp"),
            P("dp", "tensor"),
            P("dp", "tensor"),
            P("dp", "tensor"),
            P("tensor"),
            P("tensor"),
            P("tensor", "dp"),
            P(),
            P(),
            P(),
            P("dp", "tensor"),
            P("tensor"),
            P("tensor", "dp"),
            P(),
            P(),
            P(),
            P("dp", "tensor", None),
        ),
        out_specs=(
            P("dp", "tensor", None),
            P("dp", "tensor", None),
            P("dp", "tensor"),
            P("dp", "tensor"),
            P("dp", "tensor"),
            P("tensor"),
            P("tensor"),
            P("tensor", "dp"),
            P(),
            P(),
            P(),
            P("dp", "tensor"),
            P("tensor"),
            P("tensor", "dp"),
            P(),
            P(),
            P(),
        ),
        check_vma=False,
    )
```

profile of v0, /device:TPU:0, one launch (start us, length us, event | category | flops | bytes accessed | tf_op | source)
XLA Modules:
  0.0 1471.8 jit_solution(11094318295025059923)
XLA Ops:
  14.3 1180.0 %while.39 = (s32[]{:T(128)}, f32[1024,768]{1,0:T(8,128)}, f32[256,1024]{1,0:T(8,128)}, f32[1024,1024]{1,0:T(8,128)}, f32[1024,1024]{1,0:T(8,128)}, /*index=5*/f3...) while((s32[]{:T(128)}, f32[1024,768]{1,0:T(8,128)}, ...), condition=%wide.region_28.29_spmd.clone, body=%wide.region_0.28_spmd.clone.sunk | while | flops 22766163968 | bytes 654625408 | solution.py:261
  18.1 11.7 all_gather.57
  29.8 9.5 all_gather.56
  39.4 9.2 all_gather.55
  48.6 9.5 all_gather.54
  58.2 7.7 all-gather.11.cloned.1.call-done
  65.9 3.5 fusion.229
  71.2 3.0 fusion.232
  85.5 75.0 %reduce-scatter.23.cloned.1.call-done = f32[256,1024]{1,0:T(8,128)} async-done(((f32[1024,1024]{1,0:T(8,128)}), f32[256,1024]{1,0:T(8,128)}) %reduce-scatter.23.cloned.1.call-update) | async-done | bytes 1048592 | tf_op jit(solution)/shard_map/while/body/eval_jaxpr/reduce_scatter | solution.py:152
  164.5 45.0 %all-gather.13.cloned.1.call-done = bf16[1024,1024]{1,0:T(8,128)(2,1)} async-done(((bf16[256,1024]{1,0:T(8,128)(2,1)}), bf16[1024,1024]{1,0:T(8,128)(2,1)}) %all-gather.13.cloned.1.call-update) | async-done | bytes 2097168 | tf_op jit(solution)/shard_map/while/body/eval_jaxpr/all_gather | solution.py:161
  209.5 14.9 %multiply_convert_fusion.5 = (bf16[1024,1024]{1,0:T(8,128)(2,1)}, f32[1024,1024]{1,0:T(8,128)}, f32[1024,1024]{1,0:T(8,128)}) fusion(f32[1024]{0:T(1024)S(1)} %get-tuple-element.881, bf16[1024,1024]{1,0:T(8,128)(2,1)} %all-gather.13.cloned.1.call-done, bf16[1024,1024]{1,0:T(8,128)(2,1)} %all-gather.15.cloned.1.call-done), kind=kOutput, calls=%fused_computation.26.clone.1 | convolution fusion | flops 2216689664 | bytes 14684160 | tf_op jit(solution)/shard_map/while/body/eval_jaxpr/dot_general | solution.py:162
  224.4 13.8 all-gather.17.cloned.1.call-done
  238.2 6.6 fusion.240
  245.6 76.2 %reduce-scatter.25.cloned.1.call-done = f32[256,1024]{1,0:T(8,128)} async-done(((f32[1024,1024]{1,0:T(8,128)}), f32[256,1024]{1,0:T(8,128)}) %reduce-scatter.25.cloned.1.call-update) | async-done | bytes 1048592 | tf_op jit(solution)/shard_map/while/body/eval_jaxpr/reduce_scatter | solution.py:165
  330.0 46.5 %all-gather.19.cloned.1.call-done = bf16[1024,1024]{1,0:T(8,128)(2,1)} async-done(((bf16[256,1024]{1,0:T(8,128)(2,1)}), bf16[1024,1024]{1,0:T(8,128)(2,1)}) %all-gather.19.cloned.1.call-update) | async-done | bytes 2097168 | tf_op jit(solution)/shard_map/while/body/eval_jaxpr/all_gather | solution.py:179
  376.4 8.5 convert_reduce_fusion.6
  386.3 4.3 fusion.245
  390.7 75.6 %reduce-scatter.27.cloned.1.call-done = f32[256,1024]{1,0:T(8,128)} async-done(((f32[1024,1024]{1,0:T(8,128)}), f32[256,1024]{1,0:T(8,128)}) %reduce-scatter.27.cloned.1.call-update) | async-done | bytes 1048592 | tf_op jit(solution)/shard_map/while/body/eval_jaxpr/reduce_scatter | solution.py:186
  471.0 45.9 %all-gather.21.cloned.1.call-done = bf16[1024,1024]{1,0:T(8,128)(2,1)} async-done(((bf16[256,1024]{1,0:T(8,128)(2,1)}), bf16[1024,1024]{1,0:T(8,128)(2,1)}) %all-gather.21.cloned.1.call-update) | async-done | bytes 2097168 | tf_op jit(solution)/shard_map/while/body/eval_jaxpr/all_gather | solution.py:191
  519.6 5.8 fusion.249
  525.4 6.1 fusion.248
  531.6 9.1 multiply_reduce_fusion.13
  540.7 8.1 multiply_convert_fusion.6
  557.0 3.2 convolution_convert_fusion.5
  560.8 7.0 select_add_fusion.23
  567.9 4.4 select_add_fusion.22
  574.8 3.5 select_add_fusion.21
  578.3 24.3 %reduce-scatter.29.cloned.1.call-done = bf16[256,1024]{1,0:T(8,128)(2,1)} async-done(((bf16[1024,1024]{1,0:T(8,128)(2,1)}), bf16[256,1024]{1,0:T(8,128)(2,1)}) %reduce-scatter.29.cloned.1.call-update) | async-done | bytes 524304 | tf_op jit(solution)/shard_map/while/body/eval_jaxpr/reduce_scatter | solution.py:220
  609.1 10.2 all_gather.57
  619.3 9.5 all_gather.56
  628.9 9.2 all_gather.55
  638.1 9.5 all_gather.54
  647.7 5.4 all-gather.11.cloned.1.call-done
  653.1 3.5 fusion.229
  658.3 3.0 fusion.232
  672.7 75.0 %reduce-scatter.23.cloned.1.call-done = f32[256,1024]{1,0:T(8,128)} async-done(((f32[1024,1024]{1,0:T(8,128)}), f32[256,1024]{1,0:T(8,128)}) %reduce-scatter.23.cloned.1.call-update) | async-done | bytes 1048592 | tf_op jit(solution)/shard_map/while/body/eval_jaxpr/reduce_scatter | solution.py:152
  751.3 45.4 %all-gather.13.cloned.1.call-done = bf16[1024,1024]{1,0:T(8,128)(2,1)} async-done(((bf16[256,1024]{1,0:T(8,128)(2,1)}), bf16[1024,1024]{1,0:T(8,128)(2,1)}) %all-gather.13.cloned.1.call-update) | async-done | bytes 2097168 | tf_op jit(solution)/shard_map/while/body/eval_jaxpr/all_gather | solution.py:161
  796.7 14.9 %multiply_convert_fusion.5 = (bf16[1024,1024]{1,0:T(8,128)(2,1)}, f32[1024,1024]{1,0:T(8,128)}, f32[1024,1024]{1,0:T(8,128)}) fusion(f32[1024]{0:T(1024)S(1)} %get-tuple-element.881, bf16[1024,1024]{1,0:T(8,128)(2,1)} %all-gather.13.cloned.1.call-done, bf16[1024,1024]{1,0:T(8,128)(2,1)} %all-gather.15.cloned.1.call-done), kind=kOutput, calls=%fused_computation.26.clone.1 | convolution fusion | flops 2216689664 | bytes 14684160 | tf_op jit(solution)/shard_map/while/body/eval_jaxpr/dot_general | solution.py:162
  811.6 13.8 all-gather.17.cloned.1.call-done
  825.4 6.6 fusion.240
  832.8 76.2 %reduce-scatter.25.cloned.1.call-done = f32[256,1024]{1,0:T(8,128)} async-done(((f32[1024,1024]{1,0:T(8,128)}), f32[256,1024]{1,0:T(8,128)}) %reduce-scatter.25.cloned.1.call-update) | async-done | bytes 1048592 | tf_op jit(solution)/shard_map/while/body/eval_jaxpr/reduce_scatter | solution.py:165
  917.2 46.5 %all-gather.19.cloned.1.call-done = bf16[1024,1024]{1,0:T(8,128)(2,1)} async-done(((bf16[256,1024]{1,0:T(8,128)(2,1)}), bf16[1024,1024]{1,0:T(8,128)(2,1)}) %all-gather.19.cloned.1.call-update) | async-done | bytes 2097168 | tf_op jit(solution)/shard_map/while/body/eval_jaxpr/all_gather | solution.py:179
  963.6 8.5 convert_reduce_fusion.6
  973.5 4.3 fusion.245
  977.9 75.6 %reduce-scatter.27.cloned.1.call-done = f32[256,1024]{1,0:T(8,128)} async-done(((f32[1024,1024]{1,0:T(8,128)}), f32[256,1024]{1,0:T(8,128)}) %reduce-scatter.27.cloned.1.call-update) | async-done | bytes 1048592 | tf_op jit(solution)/shard_map/while/body/eval_jaxpr/reduce_scatter | solution.py:186
  1058.3 45.9 %all-gather.21.cloned.1.call-done = bf16[1024,1024]{1,0:T(8,128)(2,1)} async-done(((bf16[256,1024]{1,0:T(8,128)(2,1)}), bf16[1024,1024]{1,0:T(8,128)(2,1)}) %all-gather.21.cloned.1.call-update) | async-done | bytes 2097168 | tf_op jit(solution)/shard_map/while/body/eval_jaxpr/all_gather | solution.py:191
  1106.8 5.8 fusion.249
  1112.6 6.1 fusion.248
  1118.8 9.1 multiply_reduce_fusion.13
  1127.9 8.1 multiply_convert_fusion.6
  1144.4 3.2 convolution_convert_fusion.5
  1148.2 8.2 select_add_fusion.23
  1156.5 6.8 select_add_fusion.22
  1163.5 3.1 convolution_add_fusion.3
  1166.6 5.5 select_add_fusion.21
  1172.2 17.8 %reduce-scatter.29.cloned.1.call-done = bf16[256,1024]{1,0:T(8,128)(2,1)} async-done(((bf16[1024,1024]{1,0:T(8,128)(2,1)}), bf16[256,1024]{1,0:T(8,128)(2,1)}) %reduce-scatter.29.cloned.1.call-update) | async-done | bytes 524304 | tf_op jit(solution)/shard_map/while/body/eval_jaxpr/reduce_scatter | solution.py:220
  1195.1 3.6 fusion.73
  1201.3 14.1 all-reduce.1
  1215.4 39.5 %all-reduce = (f32[1024]{0:T(1024)}, f32[1024]{0:T(1024)}, f32[1024]{0:T(1024)}, f32[1024]{0:T(1024)}, f32[1024]{0:T(1024)}, /*index=5*/f32[1024]{0:T(1024)}) all-reduce(f32[1024]{0:T(1024)S(1)} %copy-done.28, f32[1024]{0:T(1024)S(1)} %copy-done.25, f32[1024]{0:T(1024)S(1)} %copy-done.22, ...), channel_id=1, replica_groups=mesh['dp'=8,'tensor'=4] {'dp','tensor'}, use_global_device_ids=true, to_apply=%region_35.36 | all-reduce | flops 6144 | bytes 49152 | tf_op jit(solution)/shard_map/psum | solution.py:279
  1254.9 19.2 %reduce-scatter.15.cloned.1.call-done = f32[128,256]{1,0:T(8,128)} async-done(((f32[1024,256]{1,0:T(8,128)}), f32[128,256]{1,0:T(8,128)}) %reduce-scatter.15.cloned.1.call-update) | async-done | bytes 131088 | tf_op jit(solution)/shard_map/reduce_scatter | solution.py:269
  1274.1 39.8 %reduce-scatter.11.cloned.1.call-done = f32[128,256]{1,0:T(8,128)} async-done(((f32[1024,256]{1,0:T(8,128)}), f32[128,256]{1,0:T(8,128)}) %reduce-scatter.11.cloned.1.call-update) | async-done | bytes 131088 | tf_op jit(solution)/shard_map/reduce_scatter | solution.py:265
  1313.9 39.7 %reduce-scatter.13.cloned.1.call-done = f32[128,256]{1,0:T(8,128)} async-done(((f32[1024,256]{1,0:T(8,128)}), f32[128,256]{1,0:T(8,128)}) %reduce-scatter.13.cloned.1.call-update) | async-done | bytes 131088 | tf_op jit(solution)/shard_map/reduce_scatter | solution.py:266
  1353.6 55.3 %reduce-scatter.19.cloned.1.call-done = f32[128,1024]{1,0:T(8,128)} async-done(((f32[1024,1024]{1,0:T(8,128)}), f32[128,1024]{1,0:T(8,128)}) %reduce-scatter.19.cloned.1.call-update) | async-done | bytes 524304 | tf_op jit(solution)/shard_map/reduce_scatter | solution.py:272
  1408.9 55.5 %reduce-scatter.21.cloned.1.call-done = f32[1024,128]{1,0:T(8,128)} async-done(((f32[1024,1024]{1,0:T(8,128)}), f32[1024,128]{1,0:T(8,128)}) %reduce-scatter.21.cloned.1.call-update) | async-done | bytes 524304 | tf_op jit(solution)/shard_map/reduce_scatter | solution.py:276
  (368 shorter events, 110.9 us)
Async XLA Ops:
  14.3 51.6 %all-gather.11.cloned.1.call-start = ((), (), s32[]{:S(2)}) async-start(), calls=%async_computation.16 | async-start | bytes 2621440 | tf_op jit(solution)/shard_map/while/body/eval_jaxpr/all_gather | solution.py:133
  16.2 144.3 %reduce-scatter.23.cloned.1.call-start = ((), (), s32[]{:S(2)}) async-start(), calls=%async_computation.17 | async-start | bytes 5242880 | tf_op jit(solution)/shard_map/while/body/eval_jaxpr/reduce_scatter | solution.py:152
  29.8 52.3 %copy-start.12 = (bf16[256,1024]{1,0:T(8,128)(2,1)}, bf16[256,1024]{1,0:T(8,128)(2,1)S(1)}, u32[]{:S(2)}) copy-start(bf16[256,1024]{1,0:T(8,128)(2,1)S(1)} %all_gather.57) | copy-start | bytes 1572868 | tf_op jit(solution)/shard_map/while
  58.2 11.2 copy-start.18
  69.7 10.0 copy-start.4
  71.1 8.6 copy-start
  84.8 75.7 %copy-start.13 = (bf16[2,256,1024]{2,1,0:T(8,128)(2,1)S(1)}, bf16[2,256,1024]{2,1,0:T(8,128)(2,1)}, u32[]{:S(2)}) copy-start(bf16[2,256,1024]{2,1,0:T(8,128)(2,1)} %get-tuple-element.867) | copy-start | bytes 3145732 | tf_op jit(solution)/shard_map/while
  84.9 79.6 %all-gather.15.cloned.1.call-start = ((), (), s32[]{:S(2)}) async-start(), calls=%async_computation.19 | async-start | bytes 2359296 | tf_op jit(solution)/shard_map/while/body/eval_jaxpr/all_gather | solution.py:75
  85.4 124.0 %all-gather.13.cloned.1.call-start = ((), (), s32[]{:S(2)}) async-start(), calls=%async_computation.18 | async-start | bytes 2621440 | tf_op jit(solution)/shard_map/while/body/eval_jaxpr/all_gather | solution.py:161
  163.3 74.9 %all-gather.17.cloned.1.call-start = ((), (), s32[]{:S(2)}) async-start(), calls=%async_computation.20 | async-start | bytes 2359296 | tf_op jit(solution)/shard_map/while/body/eval_jaxpr/all_gather | solution.py:79
  163.9 157.9 %reduce-scatter.25.cloned.1.call-start = ((), (), s32[]{:S(2)}) async-start(), calls=%async_computation.21 | async-start | bytes 5242880 | tf_op jit(solution)/shard_map/while/body/eval_jaxpr/reduce_scatter | solution.py:165
  244.9 131.5 %all-gather.19.cloned.1.call-start = ((), (), s32[]{:S(2)}) async-start(), calls=%async_computation.22 | async-start | bytes 2621440 | tf_op jit(solution)/shard_map/while/body/eval_jaxpr/all_gather | solution.py:179
  329.9 136.4 %reduce-scatter.27.cloned.1.call-start = ((), (), s32[]{:S(2)}) async-start(), calls=%async_computation.23 | async-start | bytes 5242880 | tf_op jit(solution)/shard_map/while/body/eval_jaxpr/reduce_scatter | solution.py:186
  376.4 9.9 copy-start.37
  390.7 126.3 %all-gather.21.cloned.1.call-start = ((), (), s32[]{:S(2)}) async-start(), calls=%async_computation.24 | async-start | bytes 2621440 | tf_op jit(solution)/shard_map/while/body/eval_jaxpr/all_gather | solution.py:191
  470.8 131.8 %reduce-scatter.29.cloned.1.call-start = ((), (), s32[]{:S(2)}) async-start(), calls=%async_computation.25 | async-start | bytes 2621440 | tf_op jit(solution)/shard_map/while/body/eval_jaxpr/reduce_scatter | solution.py:220
  517.0 14.6 slice-start.2
  519.6 12.0 slice-start
  519.6 11.9 slice-start.3
  560.8 7.0 copy-start.39
  560.8 7.0 copy-start.36
  560.8 7.0 copy-start.41
  574.8 27.8 %copy-start.3 = (f32[256,1024]{1,0:T(8,128)S(1)}, f32[256,1024]{1,0:T(8,128)}, u32[]{:S(2)}) copy-start(f32[256,1024]{1,0:T(8,128)} %copy-done.2) | copy-start | bytes 3145732 | tf_op jit(solution)/shard_map/while
  605.2 47.9 %all-gather.11.cloned.1.call-start = ((), (), s32[]{:S(2)}) async-start(), calls=%async_computation.16 | async-start | bytes 2621440 | tf_op jit(solution)/shard_map/while/body/eval_jaxpr/all_gather | solution.py:133
  607.2 140.5 %reduce-scatter.23.cloned.1.call-start = ((), (), s32[]{:S(2)}) async-start(), calls=%async_computation.17 | async-start | bytes 5242880 | tf_op jit(solution)/shard_map/while/body/eval_jaxpr/reduce_scatter | solution.py:152
  619.3 50.0 %copy-start.12 = (bf16[256,1024]{1,0:T(8,128)(2,1)}, bf16[256,1024]{1,0:T(8,128)(2,1)S(1)}, u32[]{:S(2)}) copy-start(bf16[256,1024]{1,0:T(8,128)(2,1)S(1)} %all_gather.57) | copy-start | bytes 1572868 | tf_op jit(solution)/shard_map/while
  647.7 8.9 copy-start.18
  656.9 10.0 copy-start.4
  658.3 8.6 copy-start
  672.0 75.7 %copy-start.13 = (bf16[2,256,1024]{2,1,0:T(8,128)(2,1)S(1)}, bf16[2,256,1024]{2,1,0:T(8,128)(2,1)}, u32[]{:S(2)}) copy-start(bf16[2,256,1024]{2,1,0:T(8,128)(2,1)} %get-tuple-element.867) | copy-start | bytes 3145732 | tf_op jit(solution)/shard_map/while
  672.1 79.3 %all-gather.15.cloned.1.call-start = ((), (), s32[]{:S(2)}) async-start(), calls=%async_computation.19 | async-start | bytes 2359296 | tf_op jit(solution)/shard_map/while/body/eval_jaxpr/all_gather | solution.py:75
  672.7 124.0 %all-gather.13.cloned.1.call-start = ((), (), s32[]{:S(2)}) async-start(), calls=%async_computation.18 | async-start | bytes 2621440 | tf_op jit(solution)/shard_map/while/body/eval_jaxpr/all_gather | solution.py:161
  750.5 74.9 %all-gather.17.cloned.1.call-start = ((), (), s32[]{:S(2)}) async-start(), calls=%async_computation.20 | async-start | bytes 2359296 | tf_op jit(solution)/shard_map/while/body/eval_jaxpr/all_gather | solution.py:79
  751.1 157.9 %reduce-scatter.25.cloned.1.call-start = ((), (), s32[]{:S(2)}) async-start(), calls=%async_computation.21 | async-start | bytes 5242880 | tf_op jit(solution)/shard_map/while/body/eval_jaxpr/reduce_scatter | solution.py:165
  832.1 131.5 %all-gather.19.cloned.1.call-start = ((), (), s32[]{:S(2)}) async-start(), calls=%async_computation.22 | async-start | bytes 2621440 | tf_op jit(solution)/shard_map/while/body/eval_jaxpr/all_gather | solution.py:179
  917.1 136.4 %reduce-scatter.27.cloned.1.call-start = ((), (), s32[]{:S(2)}) async-start(), calls=%async_computation.23 | async-start | bytes 5242880 | tf_op jit(solution)/shard_map/while/body/eval_jaxpr/reduce_scatter | solution.py:186
  963.6 9.9 copy-start.37
  977.9 126.3 %all-gather.21.cloned.1.call-start = ((), (), s32[]{:S(2)}) async-start(), calls=%async_computation.24 | async-start | bytes 2621440 | tf_op jit(solution)/shard_map/while/body/eval_jaxpr/all_gather | solution.py:191
  1058.0 132.0 %reduce-scatter.29.cloned.1.call-start = ((), (), s32[]{:S(2)}) async-start(), calls=%async_computation.25 | async-start | bytes 2621440 | tf_op jit(solution)/shard_map/while/body/eval_jaxpr/reduce_scatter | solution.py:220
  1104.2 14.6 slice-start.2
  1106.8 12.0 slice-start
  1106.8 11.9 slice-start.3
  1148.2 8.2 copy-start.39
  1148.2 8.2 copy-start.36
  1148.2 8.2 copy-start.41
  1156.4 6.8 copy-start.20
  1156.4 7.1 copy-start.29
  1156.4 7.0 copy-start.32
  1156.5 7.1 copy-start.11
  1163.2 8.9 copy-start.27
  1163.3 8.9 copy-start.21
  1163.3 8.9 copy-start.24
  1163.5 8.7 copy-start.30
  1163.5 8.7 copy-start.33
  1166.6 23.4 %copy-start.3 = (f32[256,1024]{1,0:T(8,128)S(1)}, f32[256,1024]{1,0:T(8,128)}, u32[]{:S(2)}) copy-start(f32[256,1024]{1,0:T(8,128)} %copy-done.2) | copy-start | bytes 3145732 | tf_op jit(solution)/shard_map/while
  1194.3 60.7 %reduce-scatter.17.cloned.1.call-start = ((), (), s32[]{:S(2)}) async-start(), calls=%async_computation.13 | async-start | bytes 1179648 | tf_op jit(solution)/shard_map/reduce_scatter | solution.py:275
  1195.0 79.1 %reduce-scatter.15.cloned.1.call-start = ((), (), s32[]{:S(2)}) async-start(), calls=%async_computation.12 | async-start | bytes 1179648 | tf_op jit(solution)/shard_map/reduce_scatter | solution.py:269
  1198.7 115.3 %reduce-scatter.11.cloned.1.call-start = ((), (), s32[]{:S(2)}) async-start(), calls=%async_computation.10 | async-start | bytes 1179648 | tf_op jit(solution)/shard_map/reduce_scatter | solution.py:265
  1199.4 154.2 %reduce-scatter.13.cloned.1.call-start = ((), (), s32[]{:S(2)}) async-start(), calls=%async_computation.11 | async-start | bytes 1179648 | tf_op jit(solution)/shard_map/reduce_scatter | solution.py:266
  1200.0 208.9 %reduce-scatter.19.cloned.1.call-start = ((), (), s32[]{:S(2)}) async-start(), calls=%async_computation.14 | async-start | bytes 4718592 | tf_op jit(solution)/shard_map/reduce_scatter | solution.py:272
  1200.1 15.4 %copy-start.22 = (f32[1024]{0:T(1024)S(1)}, f32[1024]{0:T(1024)}, u32[]{:S(2)}) copy-start(f32[1024]{0:T(1024)} %get-tuple-element.216) | copy-start | bytes 12292
  1200.1 15.3 %copy-start.25 = (f32[1024]{0:T(1024)S(1)}, f32[1024]{0:T(1024)}, u32[]{:S(2)}) copy-start(f32[1024]{0:T(1024)} %get-tuple-element.215) | copy-start | bytes 12292
  1200.1 15.3 %copy-start.28 = (f32[1024]{0:T(1024)S(1)}, f32[1024]{0:T(1024)}, u32[]{:S(2)}) copy-start(f32[1024]{0:T(1024)} %get-tuple-element.214) | copy-start | bytes 12292
  1200.7 263.7 %reduce-scatter.21.cloned.1.call-start = ((), (), s32[]{:S(2)}) async-start(), calls=%async_computation.15 | async-start | bytes 4718592 | tf_op jit(solution)/shard_map/reduce_scatter | solution.py:276
  (49 other events, 162.8 us)
Sparse Core Ops, SparseCore 0:
  17.2 48.6 all-gather.10
  85.0 75.4 reduce-scatter.22
  330.1 46.3 all-gather.18
  390.8 75.4 reduce-scatter.26
  607.9 45.1 all-gather.10
  672.2 75.4 reduce-scatter.22
  917.3 46.3 all-gather.18
  978.0 75.4 reduce-scatter.26
  1198.9 35.5 reduce-scatter.16
  1238.1 36.0 reduce-scatter.14
  1277.9 36.0 reduce-scatter.10
  1317.5 36.0 reduce-scatter.12
  1357.5 51.2 reduce-scatter.18
  1413.0 51.3 reduce-scatter.20
Sparse Core Ops, SparseCore 1:
  87.2 26.4 all-gather.14
  163.4 46.0 all-gather.12
  211.4 26.8 all-gather.16
  245.0 76.7 reduce-scatter.24
  470.9 46.0 all-gather.20
  560.3 42.3 reduce-scatter.28
  674.4 26.4 all-gather.14
  750.6 46.0 all-gather.12
  798.6 26.8 all-gather.16
  832.2 76.7 reduce-scatter.24
  1058.1 46.0 all-gather.20
  1147.7 42.3 reduce-scatter.28
where the time goes:
time: 1470 us
  waiting for transfers between devices  1030 us (70%)
  matrix products  206 us (14%)
  blocking collectives  132 us (9%)
  other arithmetic  63.6 us (4%)
  local copies, waits for them, and re-layouts  21.4 us (1%)
  between operations  15.7 us (1%)
    reduce_scatter x2, waiting for transfers between devices, one_batch(): lax.psum_scatter(jnp.dot(hidden_low, matrix_back, preferred_element_type=...  152 us
    reduce_scatter x2, waiting for transfers between devices, one_batch(): lax.psum_scatter(contract_cols(grad_pre_low, matrix_in), 'tensor', scatte...  151 us
    reduce_scatter x2, waiting for transfers between devices, one_batch(): lax.psum_scatter(jnp.dot(context_low, matrix_out, preferred_element_type=...  150 us
    all_gather x2, waiting for transfers between devices, one_batch(): lax.all_gather(grad_mixed.astype(bf16), 'tensor', axis=0, tiled=True)  92.9 us
    all_gather x2, waiting for transfers between devices, one_batch(): lax.all_gather(grad_att.astype(bf16), 'tensor', axis=0, tiled=True)  91.8 us
    all_gather x2, waiting for transfers between devices, one_batch(): full_first = lax.all_gather(first_low, 'tensor', axis=0, tiled=True)  90.3 us
    reduce_scatter x1, waiting for transfers between devices, on_device(): lax.psum_scatter(totals[3], 'dp', scatter_dimension=1, tiled=True)  55.5 us
    reduce_scatter x1, waiting for transfers between devices, on_device(): lax.psum_scatter(totals[2], 'dp', scatter_dimension=0, tiled=True)  55.3 us
  transfers between devices with their start and end apart: 26, of which 23 were waited for; matrix products, arithmetic and copies ran while one was open for 6% of the time, Pallas kernels for 0%

commit v1 on v0

--- a/solution.py
+++ b/solution.py
@@ -188,7 +188,16 @@
         )
         grad_first = grad_mixed + grad_first_mix
         grad_att, grad_gain_a, grad_shift_a = first_back(grad_first)
-        full_grad_att = lax.all_gather(grad_att.astype(bf16), "tensor", axis=0, tiled=True)
+        field = grad_att.astype(bf16)
+        full_grad_att = jnp.concatenate(
+            jax.lax.all_to_all(
+                jnp.stack([field for _ in range(jax.lax.axis_size("tensor"))], axis=0),
+                "tensor",
+                0,
+                0,
+            ),
+            axis=0,
+        )
         grad_context = contract_cols(full_grad_att, matrix_out).astype(bf16)
         grad_out_w = contract_rows(context_low, full_grad_att)
         grad_context_heads = grad_context.reshape(slots, local_heads, HD)

time: 1470 us -> 1500 us (1.020)
    all_to_all x0 -> x2, waiting for transfers between devices: none -> 97.1 us  [one_batch(): jax.lax.all_to_all(jnp.stack([field for _ in range(jax.lax.axis_size('ten...]
    all_gather x2 -> x0, waiting for transfers between devices: 91.8 us -> none  [one_batch(): lax.all_gather(grad_att.astype(bf16), 'tensor', axis=0, tiled=True)]
where the time goes in v1:
time: 1500 us
  waiting for transfers between devices  1020 us (68%)
  matrix products  213 us (14%)
  blocking collectives  132 us (9%)
  other arithmetic  66.2 us (4%)
  local copies, waits for them, and re-layouts  30 us (2%)
  between operations  16.2 us (1%)
    reduce_scatter x2, waiting for transfers between devices, one_batch(): lax.psum_scatter(jnp.dot(hidden_low, matrix_back, preferred_element_type=...  152 us
    reduce_scatter x2, waiting for transfers between devices, one_batch(): lax.psum_scatter(contract_cols(grad_pre_low, matrix_in), 'tensor', scatte...  151 us
    reduce_scatter x2, waiting for transfers between devices, one_batch(): lax.psum_scatter(jnp.dot(context_low, matrix_out, preferred_element_type=...  150 us
    all_to_all x2, waiting for transfers between devices, one_batch(): jax.lax.all_to_all(jnp.stack([field for _ in range(jax.lax.axis_size('ten...  97.1 us
    all_gather x2, waiting for transfers between devices, one_batch(): lax.all_gather(grad_mixed.astype(bf16), 'tensor', axis=0, tiled=True)  92.1 us
    all_gather x2, waiting for transfers between devices, one_batch(): full_first = lax.all_gather(first_low, 'tensor', axis=0, tiled=True)  90.5 us
    reduce_scatter x1, waiting for transfers between devices, on_device(): lax.psum_scatter(totals[3], 'dp', scatter_dimension=1, tiled=True)  55.5 us
    reduce_scatter x1, waiting for transfers between devices, on_device(): lax.psum_scatter(totals[2], 'dp', scatter_dimension=0, tiled=True)  55.2 us
  transfers between devices with their start and end apart: 26, of which 23 were waited for; matrix products, arithmetic and copies ran while one was open for 6% of the time, Pallas kernels for 0%

profile of v1, /device:TPU:0, one launch (start us, length us, event | category | flops | bytes accessed | tf_op | source)
XLA Modules:
  0.0 1496.5 jit_solution(2582315591460883887)
XLA Ops:
  16.6 1202.5 %while.39 = (s32[]{:T(128)}, f32[1024,768]{1,0:T(8,128)}, f32[256,1024]{1,0:T(8,128)}, f32[1024,1024]{1,0:T(8,128)}, f32[1024,1024]{1,0:T(8,128)}, /*index=5*/f3...) while((s32[]{:T(128)}, f32[1024,768]{1,0:T(8,128)}, ...), condition=%wide.region_28.29_spmd.clone, body=%wide.region_0.28_spmd.clone.sunk | while | flops 22767212544 | bytes 648753792 | solution.py:270
  20.5 11.7 all_gather.52
  32.3 9.5 all_gather.51
  41.8 9.2 all_gather.50
  51.0 9.5 all_gather.49
  63.1 5.2 all-gather.10.cloned.1.call-done
  68.3 3.9 fusion.230
  74.7 3.0 fusion.233
  89.1 75.0 %reduce-scatter.23.cloned.1.call-done = f32[256,1024]{1,0:T(8,128)} async-done(((f32[1024,1024]{1,0:T(8,128)}), f32[256,1024]{1,0:T(8,128)}) %reduce-scatter.23.cloned.1.call-update) | async-done | bytes 1048592 | tf_op jit(solution)/shard_map/while/body/eval_jaxpr/reduce_scatter | solution.py:152
  168.0 45.2 %all-gather.12.cloned.1.call-done = bf16[1024,1024]{1,0:T(8,128)(2,1)} async-done(((bf16[256,1024]{1,0:T(8,128)(2,1)}), bf16[1024,1024]{1,0:T(8,128)(2,1)}) %all-gather.12.cloned.1.call-update) | async-done | bytes 2097168 | tf_op jit(solution)/shard_map/while/body/eval_jaxpr/all_gather | solution.py:161
  213.1 15.0 %multiply_convert_fusion.5 = (bf16[1024,1024]{1,0:T(8,128)(2,1)}, f32[1024,1024]{1,0:T(8,128)}, f32[1024,1024]{1,0:T(8,128)}) fusion(f32[1024]{0:T(1024)S(1)} %get-tuple-element.881, bf16[1024,1024]{1,0:T(8,128)(2,1)} %all-gather.12.cloned.1.call-done, bf16[1024,1024]{1,0:T(8,128)(2,1)} %all-gather.14.cloned.1.call-done), kind=kOutput, calls=%fused_computation.26.clone.1 | convolution fusion | flops 2216689664 | bytes 14684160 | tf_op jit(solution)/shard_map/while/body/eval_jaxpr/dot_general | solution.py:162
  228.2 13.7 all-gather.16.cloned.1.call-done
  241.9 6.6 fusion.241
  249.3 76.2 %reduce-scatter.25.cloned.1.call-done = f32[256,1024]{1,0:T(8,128)} async-done(((f32[1024,1024]{1,0:T(8,128)}), f32[256,1024]{1,0:T(8,128)}) %reduce-scatter.25.cloned.1.call-update) | async-done | bytes 1048592 | tf_op jit(solution)/shard_map/while/body/eval_jaxpr/reduce_scatter | solution.py:165
  334.3 45.9 %all-gather.18.cloned.1.call-done = bf16[1024,1024]{1,0:T(8,128)(2,1)} async-done(((bf16[256,1024]{1,0:T(8,128)(2,1)}), bf16[1024,1024]{1,0:T(8,128)(2,1)}) %all-gather.18.cloned.1.call-update) | async-done | bytes 2097168 | tf_op jit(solution)/shard_map/while/body/eval_jaxpr/all_gather | solution.py:179
  380.2 9.1 convert_reduce_fusion.6
  390.6 4.4 fusion.246
  395.0 75.6 %reduce-scatter.27.cloned.1.call-done = f32[256,1024]{1,0:T(8,128)} async-done(((f32[1024,1024]{1,0:T(8,128)}), f32[256,1024]{1,0:T(8,128)}) %reduce-scatter.27.cloned.1.call-update) | async-done | bytes 1048592 | tf_op jit(solution)/shard_map/while/body/eval_jaxpr/reduce_scatter | solution.py:186
  477.1 4.5 all-to-all-start
  481.8 48.6 %all-to-all-done = bf16[4,256,1024]{2,1,0:T(8,128)(2,1)} async-done(((bf16[4,256,1024]{2,1,0:T(8,128)(2,1)}), bf16[4,256,1024]{2,1,0:T(8,128)(2,1)}, u32[]{:S(2)}, u32[]{:S(2)}) %all-to-all-start) | async-done | bytes 2097184 | tf_op jit(solution)/shard_map/while/body/eval_jaxpr/all_to_all | solution.py:193
  533.0 5.5 fusion.250
  538.5 6.1 fusion.249
  544.6 8.6 multiply_reduce_fusion.13
  553.3 8.1 multiply_convert_fusion.6
  569.0 4.8 convolution_convert_fusion.5
  574.6 6.9 select_add_fusion.23
  581.7 4.5 select_add_fusion.22
  589.3 5.1 select_add_fusion.21
  594.4 21.7 %reduce-scatter.29.cloned.1.call-done = bf16[256,1024]{1,0:T(8,128)(2,1)} async-done(((bf16[1024,1024]{1,0:T(8,128)(2,1)}), bf16[256,1024]{1,0:T(8,128)(2,1)}) %reduce-scatter.29.cloned.1.call-update) | async-done | bytes 524304 | tf_op jit(solution)/shard_map/while/body/eval_jaxpr/reduce_scatter | solution.py:229
  622.7 10.2 all_gather.52
  632.9 9.5 all_gather.51
  642.4 9.2 all_gather.50
  651.6 9.5 all_gather.49
  666.7 3.9 fusion.230
  673.0 3.0 fusion.233
  687.7 74.8 %reduce-scatter.23.cloned.1.call-done = f32[256,1024]{1,0:T(8,128)} async-done(((f32[1024,1024]{1,0:T(8,128)}), f32[256,1024]{1,0:T(8,128)}) %reduce-scatter.23.cloned.1.call-update) | async-done | bytes 1048592 | tf_op jit(solution)/shard_map/while/body/eval_jaxpr/reduce_scatter | solution.py:152
  766.2 45.4 %all-gather.12.cloned.1.call-done = bf16[1024,1024]{1,0:T(8,128)(2,1)} async-done(((bf16[256,1024]{1,0:T(8,128)(2,1)}), bf16[1024,1024]{1,0:T(8,128)(2,1)}) %all-gather.12.cloned.1.call-update) | async-done | bytes 2097168 | tf_op jit(solution)/shard_map/while/body/eval_jaxpr/all_gather | solution.py:161
  811.5 15.0 %multiply_convert_fusion.5 = (bf16[1024,1024]{1,0:T(8,128)(2,1)}, f32[1024,1024]{1,0:T(8,128)}, f32[1024,1024]{1,0:T(8,128)}) fusion(f32[1024]{0:T(1024)S(1)} %get-tuple-element.881, bf16[1024,1024]{1,0:T(8,128)(2,1)} %all-gather.12.cloned.1.call-done, bf16[1024,1024]{1,0:T(8,128)(2,1)} %all-gather.14.cloned.1.call-done), kind=kOutput, calls=%fused_computation.26.clone.1 | convolution fusion | flops 2216689664 | bytes 14684160 | tf_op jit(solution)/shard_map/while/body/eval_jaxpr/dot_general | solution.py:162
  826.5 13.7 all-gather.16.cloned.1.call-done
  840.3 6.6 fusion.241
  847.6 76.2 %reduce-scatter.25.cloned.1.call-done = f32[256,1024]{1,0:T(8,128)} async-done(((f32[1024,1024]{1,0:T(8,128)}), f32[256,1024]{1,0:T(8,128)}) %reduce-scatter.25.cloned.1.call-update) | async-done | bytes 1048592 | tf_op jit(solution)/shard_map/while/body/eval_jaxpr/reduce_scatter | solution.py:165
  932.3 46.2 %all-gather.18.cloned.1.call-done = bf16[1024,1024]{1,0:T(8,128)(2,1)} async-done(((bf16[256,1024]{1,0:T(8,128)(2,1)}), bf16[1024,1024]{1,0:T(8,128)(2,1)}) %all-gather.18.cloned.1.call-update) | async-done | bytes 2097168 | tf_op jit(solution)/shard_map/while/body/eval_jaxpr/all_gather | solution.py:179
  978.5 9.1 convert_reduce_fusion.6
  989.0 4.4 fusion.246
  993.4 75.6 %reduce-scatter.27.cloned.1.call-done = f32[256,1024]{1,0:T(8,128)} async-done(((f32[1024,1024]{1,0:T(8,128)}), f32[256,1024]{1,0:T(8,128)}) %reduce-scatter.27.cloned.1.call-update) | async-done | bytes 1048592 | tf_op jit(solution)/shard_map/while/body/eval_jaxpr/reduce_scatter | solution.py:186
  1075.4 4.5 all-to-all-start
  1080.3 48.5 %all-to-all-done = bf16[4,256,1024]{2,1,0:T(8,128)(2,1)} async-done(((bf16[4,256,1024]{2,1,0:T(8,128)(2,1)}), bf16[4,256,1024]{2,1,0:T(8,128)(2,1)}, u32[]{:S(2)}, u32[]{:S(2)}) %all-to-all-start) | async-done | bytes 2097184 | tf_op jit(solution)/shard_map/while/body/eval_jaxpr/all_to_all | solution.py:193
  1131.4 5.5 fusion.250
  1136.8 6.1 fusion.249
  1143.0 8.6 multiply_reduce_fusion.13
  1151.6 8.1 multiply_convert_fusion.6
  1167.6 4.8 convolution_convert_fusion.5
  1173.2 8.2 select_add_fusion.23
  1181.5 6.8 select_add_fusion.22
  1191.4 6.2 select_add_fusion.21
  1197.6 17.1 %reduce-scatter.29.cloned.1.call-done = bf16[256,1024]{1,0:T(8,128)(2,1)} async-done(((bf16[1024,1024]{1,0:T(8,128)(2,1)}), bf16[256,1024]{1,0:T(8,128)(2,1)}) %reduce-scatter.29.cloned.1.call-update) | async-done | bytes 524304 | tf_op jit(solution)/shard_map/while/body/eval_jaxpr/reduce_scatter | solution.py:229
  1219.8 3.7 fusion.75
  1226.3 14.1 all-reduce.1
  1240.4 39.6 %all-reduce = (f32[1024]{0:T(1024)}, f32[1024]{0:T(1024)}, f32[1024]{0:T(1024)}, f32[1024]{0:T(1024)}, f32[1024]{0:T(1024)}, /*index=5*/f32[1024]{0:T(1024)}) all-reduce(f32[1024]{0:T(1024)S(1)} %copy-done.62, f32[1024]{0:T(1024)S(1)} %copy-done.59, f32[1024]{0:T(1024)S(1)} %copy-done.56, ...), channel_id=1, replica_groups=mesh['dp'=8,'tensor'=4] {'dp','tensor'}, use_global_device_ids=true, to_apply=%region_35.36 | all-reduce | flops 6144 | bytes 49152 | tf_op jit(solution)/shard_map/psum | solution.py:288
  1280.0 18.6 %reduce-scatter.15.cloned.1.call-done = f32[128,256]{1,0:T(8,128)} async-done(((f32[1024,256]{1,0:T(8,128)}), f32[128,256]{1,0:T(8,128)}) %reduce-scatter.15.cloned.1.call-update) | async-done | bytes 131088 | tf_op jit(solution)/shard_map/reduce_scatter | solution.py:278
  1298.6 39.6 %reduce-scatter.11.cloned.1.call-done = f32[128,256]{1,0:T(8,128)} async-done(((f32[1024,256]{1,0:T(8,128)}), f32[128,256]{1,0:T(8,128)}) %reduce-scatter.11.cloned.1.call-update) | async-done | bytes 131088 | tf_op jit(solution)/shard_map/reduce_scatter | solution.py:274
  1338.2 39.7 %reduce-scatter.13.cloned.1.call-done = f32[128,256]{1,0:T(8,128)} async-done(((f32[1024,256]{1,0:T(8,128)}), f32[128,256]{1,0:T(8,128)}) %reduce-scatter.13.cloned.1.call-update) | async-done | bytes 131088 | tf_op jit(solution)/shard_map/reduce_scatter | solution.py:275
  1378.0 55.2 %reduce-scatter.19.cloned.1.call-done = f32[128,1024]{1,0:T(8,128)} async-done(((f32[1024,1024]{1,0:T(8,128)}), f32[128,1024]{1,0:T(8,128)}) %reduce-scatter.19.cloned.1.call-update) | async-done | bytes 524304 | tf_op jit(solution)/shard_map/reduce_scatter | solution.py:281
  1433.1 55.5 %reduce-scatter.21.cloned.1.call-done = f32[1024,128]{1,0:T(8,128)} async-done(((f32[1024,1024]{1,0:T(8,128)}), f32[1024,128]{1,0:T(8,128)}) %reduce-scatter.21.cloned.1.call-update) | async-done | bytes 524304 | tf_op jit(solution)/shard_map/reduce_scatter | solution.py:285
  (516 shorter events, 129.2 us)
Async XLA Ops:
  16.6 308.8 %copy-start.27 = (f32[1024]{0:T(1024)}, f32[1024]{0:T(1024)S(1)}, u32[]{:S(2)}) copy-start(f32[1024]{0:T(1024)S(1)} %get-tuple-element.879) | copy-start | bytes 12292 | tf_op jit(solution)/shard_map/while
  16.6 308.8 %copy-start.39 = (f32[1024]{0:T(1024)}, f32[1024]{0:T(1024)S(1)}, u32[]{:S(2)}) copy-start(f32[1024]{0:T(1024)S(1)} %get-tuple-element.883) | copy-start | bytes 12292 | tf_op jit(solution)/shard_map/while
  16.6 312.9 %copy-start.23 = (f32[1024]{0:T(1024)}, f32[1024]{0:T(1024)S(1)}, u32[]{:S(2)}) copy-start(f32[1024]{0:T(1024)S(1)} %get-tuple-element.874) | copy-start | bytes 12292 | tf_op jit(solution)/shard_map/while
  16.6 363.5 %copy-start.72 = (f32[1024]{0:T(1024)}, f32[1024]{0:T(1024)S(1)}, u32[]{:S(2)}) copy-start(f32[1024]{0:T(1024)S(1)} %get-tuple-element.881) | copy-start | bytes 12292 | tf_op jit(solution)/shard_map/while
  16.6 51.7 %all-gather.10.cloned.1.call-start = ((), (), s32[]{:S(2)}) async-start(), calls=%async_computation.17 | async-start | bytes 2621440 | tf_op jit(solution)/shard_map/while/body/eval_jaxpr/all_gather | solution.py:133
  18.6 145.6 %reduce-scatter.23.cloned.1.call-start = ((), (), s32[]{:S(2)}) async-start(), calls=%async_computation.18 | async-start | bytes 5242880 | tf_op jit(solution)/shard_map/while/body/eval_jaxpr/reduce_scatter | solution.py:152
  88.5 75.7 %copy-start.20 = (bf16[2,256,1024]{2,1,0:T(8,128)(2,1)S(1)}, bf16[2,256,1024]{2,1,0:T(8,128)(2,1)}, u32[]{:S(2)}) copy-start(bf16[2,256,1024]{2,1,0:T(8,128)(2,1)} %get-tuple-element.867) | copy-start | bytes 3145732 | tf_op jit(solution)/shard_map/while
  88.5 79.4 %all-gather.14.cloned.1.call-start = ((), (), s32[]{:S(2)}) async-start(), calls=%async_computation.20 | async-start | bytes 2359296 | tf_op jit(solution)/shard_map/while/body/eval_jaxpr/all_gather | solution.py:75
  89.1 124.1 %all-gather.12.cloned.1.call-start = ((), (), s32[]{:S(2)}) async-start(), calls=%async_computation.19 | async-start | bytes 2621440 | tf_op jit(solution)/shard_map/while/body/eval_jaxpr/all_gather | solution.py:161
  167.0 74.9 %all-gather.16.cloned.1.call-start = ((), (), s32[]{:S(2)}) async-start(), calls=%async_computation.21 | async-start | bytes 2359296 | tf_op jit(solution)/shard_map/while/body/eval_jaxpr/all_gather | solution.py:79
  167.5 157.9 %reduce-scatter.25.cloned.1.call-start = ((), (), s32[]{:S(2)}) async-start(), calls=%async_computation.22 | async-start | bytes 5242880 | tf_op jit(solution)/shard_map/while/body/eval_jaxpr/reduce_scatter | solution.py:165
  248.6 131.6 %all-gather.18.cloned.1.call-start = ((), (), s32[]{:S(2)}) async-start(), calls=%async_computation.23 | async-start | bytes 2621440 | tf_op jit(solution)/shard_map/while/body/eval_jaxpr/all_gather | solution.py:179
  249.3 81.8 %copy-start.63 = (pred[256]{0:T(512)(128)(4,1)}, pred[256]{0:T(512)(128)(4,1)S(1)}, u32[]{:S(2)}) copy-start(pred[256]{0:T(512)(128)(4,1)S(1)} %add_compare_fusion.2) | copy-start | bytes 772 | tf_op jit(solution)/shard_map/while
  327.1 62.1 %copy-start.25 = (f32[256]{0:T(256)}, f32[256]{0:T(256)S(1)}, u32[]{:S(2)}) copy-start(f32[256]{0:T(256)S(1)} %broadcast_multiply_fusion.5) | copy-start | bytes 3076 | tf_op jit(solution)/shard_map/while
  327.4 61.8 %copy-start.33 = (f32[256]{0:T(256)}, f32[256]{0:T(256)S(1)}, u32[]{:S(2)}) copy-start(f32[256]{0:T(256)S(1)} %fusion.243) | copy-start | bytes 3076 | tf_op jit(solution)/shard_map/while
  333.7 137.0 %reduce-scatter.27.cloned.1.call-start = ((), (), s32[]{:S(2)}) async-start(), calls=%async_computation.24 | async-start | bytes 5242880 | tf_op jit(solution)/shard_map/while/body/eval_jaxpr/reduce_scatter | solution.py:186
  477.1 53.3 %all-to-all-start = ((bf16[4,256,1024]{2,1,0:T(8,128)(2,1)}), bf16[4,256,1024]{2,1,0:T(8,128)(2,1)}, u32[]{:S(2)}, u32[]{:S(2)}) async-start(bf16[4,256,1024]{2,1,0:T(8,128)(2,1)} %stack.4), calls=%async_computation.3 | async-start | bytes 4194304 | tf_op jit(solution)/shard_map/while/body/eval_jaxpr/all_to_all | solution.py:193
  481.5 51.4 %copy-start.6 = (bf16[1024,256]{0,1:T(8,128)(2,1)S(1)}, bf16[1024,256]{0,1:T(8,128)(2,1)}, u32[]{:S(2)}) copy-start(bf16[1024,256]{0,1:T(8,128)(2,1)} %copy-done.5) | copy-start | bytes 1572868 | tf_op jit(solution)/shard_map/while
  481.6 134.6 %reduce-scatter.29.cloned.1.call-start = ((), (), s32[]{:S(2)}) async-start(), calls=%async_computation.25 | async-start | bytes 2621440 | tf_op jit(solution)/shard_map/while/body/eval_jaxpr/reduce_scatter | solution.py:229
  530.4 14.2 slice-start.2
  533.0 11.6 slice-start
  589.2 26.9 %copy-start.3 = (f32[256,1024]{1,0:T(8,128)S(1)}, f32[256,1024]{1,0:T(8,128)}, u32[]{:S(2)}) copy-start(f32[256,1024]{1,0:T(8,128)} %copy-done.2) | copy-start | bytes 3145732 | tf_op jit(solution)/shard_map/while
  589.2 26.9 %copy-start.38 = (f32[256]{0:T(256)S(1)}, f32[256]{0:T(256)}, u32[]{:S(2)}) copy-start(f32[256]{0:T(256)} %copy-done.37) | copy-start | bytes 3076 | tf_op jit(solution)/shard_map/while
  589.2 29.1 %copy-start.28 = (f32[1024]{0:T(1024)S(1)}, f32[1024]{0:T(1024)}, u32[]{:S(2)}) copy-start(f32[1024]{0:T(1024)} %copy-done.27) | copy-start | bytes 12292 | tf_op jit(solution)/shard_map/while
  589.2 29.1 %copy-start.40 = (f32[1024]{0:T(1024)S(1)}, f32[1024]{0:T(1024)}, u32[]{:S(2)}) copy-start(f32[1024]{0:T(1024)} %copy-done.39) | copy-start | bytes 12292 | tf_op jit(solution)/shard_map/while
  589.2 29.1 %copy-start.73 = (f32[1024]{0:T(1024)S(1)}, f32[1024]{0:T(1024)}, u32[]{:S(2)}) copy-start(f32[1024]{0:T(1024)} %copy-done.72) | copy-start | bytes 12292 | tf_op jit(solution)/shard_map/while
  618.8 305.0 %copy-start.27 = (f32[1024]{0:T(1024)}, f32[1024]{0:T(1024)S(1)}, u32[]{:S(2)}) copy-start(f32[1024]{0:T(1024)S(1)} %get-tuple-element.879) | copy-start | bytes 12292 | tf_op jit(solution)/shard_map/while
  618.8 305.0 %copy-start.39 = (f32[1024]{0:T(1024)}, f32[1024]{0:T(1024)S(1)}, u32[]{:S(2)}) copy-start(f32[1024]{0:T(1024)S(1)} %get-tuple-element.883) | copy-start | bytes 12292 | tf_op jit(solution)/shard_map/while
  618.8 309.1 %copy-start.23 = (f32[1024]{0:T(1024)}, f32[1024]{0:T(1024)S(1)}, u32[]{:S(2)}) copy-start(f32[1024]{0:T(1024)S(1)} %get-tuple-element.874) | copy-start | bytes 12292 | tf_op jit(solution)/shard_map/while
  618.8 359.7 %copy-start.72 = (f32[1024]{0:T(1024)}, f32[1024]{0:T(1024)S(1)}, u32[]{:S(2)}) copy-start(f32[1024]{0:T(1024)S(1)} %get-tuple-element.881) | copy-start | bytes 12292 | tf_op jit(solution)/shard_map/while
  618.8 47.8 %all-gather.10.cloned.1.call-start = ((), (), s32[]{:S(2)}) async-start(), calls=%async_computation.17 | async-start | bytes 2621440 | tf_op jit(solution)/shard_map/while/body/eval_jaxpr/all_gather | solution.py:133
  620.8 141.7 %reduce-scatter.23.cloned.1.call-start = ((), (), s32[]{:S(2)}) async-start(), calls=%async_computation.18 | async-start | bytes 5242880 | tf_op jit(solution)/shard_map/while/body/eval_jaxpr/reduce_scatter | solution.py:152
  686.8 75.7 %copy-start.20 = (bf16[2,256,1024]{2,1,0:T(8,128)(2,1)S(1)}, bf16[2,256,1024]{2,1,0:T(8,128)(2,1)}, u32[]{:S(2)}) copy-start(bf16[2,256,1024]{2,1,0:T(8,128)(2,1)} %get-tuple-element.867) | copy-start | bytes 3145732 | tf_op jit(solution)/shard_map/while
  686.9 79.3 %all-gather.14.cloned.1.call-start = ((), (), s32[]{:S(2)}) async-start(), calls=%async_computation.20 | async-start | bytes 2359296 | tf_op jit(solution)/shard_map/while/body/eval_jaxpr/all_gather | solution.py:75
  687.6 123.9 %all-gather.12.cloned.1.call-start = ((), (), s32[]{:S(2)}) async-start(), calls=%async_computation.19 | async-start | bytes 2621440 | tf_op jit(solution)/shard_map/while/body/eval_jaxpr/all_gather | solution.py:161
  765.3 75.0 %all-gather.16.cloned.1.call-start = ((), (), s32[]{:S(2)}) async-start(), calls=%async_computation.21 | async-start | bytes 2359296 | tf_op jit(solution)/shard_map/while/body/eval_jaxpr/all_gather | solution.py:79
  765.9 157.9 %reduce-scatter.25.cloned.1.call-start = ((), (), s32[]{:S(2)}) async-start(), calls=%async_computation.22 | async-start | bytes 5242880 | tf_op jit(solution)/shard_map/while/body/eval_jaxpr/reduce_scatter | solution.py:165
  846.9 131.6 %all-gather.18.cloned.1.call-start = ((), (), s32[]{:S(2)}) async-start(), calls=%async_computation.23 | async-start | bytes 2621440 | tf_op jit(solution)/shard_map/while/body/eval_jaxpr/all_gather | solution.py:179
  847.6 81.8 %copy-start.63 = (pred[256]{0:T(512)(128)(4,1)}, pred[256]{0:T(512)(128)(4,1)S(1)}, u32[]{:S(2)}) copy-start(pred[256]{0:T(512)(128)(4,1)S(1)} %add_compare_fusion.2) | copy-start | bytes 772 | tf_op jit(solution)/shard_map/while
  925.5 62.1 %copy-start.25 = (f32[256]{0:T(256)}, f32[256]{0:T(256)S(1)}, u32[]{:S(2)}) copy-start(f32[256]{0:T(256)S(1)} %broadcast_multiply_fusion.5) | copy-start | bytes 3076 | tf_op jit(solution)/shard_map/while
  925.7 61.8 %copy-start.33 = (f32[256]{0:T(256)}, f32[256]{0:T(256)S(1)}, u32[]{:S(2)}) copy-start(f32[256]{0:T(256)S(1)} %fusion.243) | copy-start | bytes 3076 | tf_op jit(solution)/shard_map/while
  932.0 137.0 %reduce-scatter.27.cloned.1.call-start = ((), (), s32[]{:S(2)}) async-start(), calls=%async_computation.24 | async-start | bytes 5242880 | tf_op jit(solution)/shard_map/while/body/eval_jaxpr/reduce_scatter | solution.py:186
  1075.4 53.3 %all-to-all-start = ((bf16[4,256,1024]{2,1,0:T(8,128)(2,1)}), bf16[4,256,1024]{2,1,0:T(8,128)(2,1)}, u32[]{:S(2)}, u32[]{:S(2)}) async-start(bf16[4,256,1024]{2,1,0:T(8,128)(2,1)} %stack.4), calls=%async_computation.3 | async-start | bytes 4194304 | tf_op jit(solution)/shard_map/while/body/eval_jaxpr/all_to_all | solution.py:193
  1079.9 51.4 %copy-start.6 = (bf16[1024,256]{0,1:T(8,128)(2,1)S(1)}, bf16[1024,256]{0,1:T(8,128)(2,1)}, u32[]{:S(2)}) copy-start(bf16[1024,256]{0,1:T(8,128)(2,1)} %copy-done.5) | copy-start | bytes 1572868 | tf_op jit(solution)/shard_map/while
  1079.9 134.8 %reduce-scatter.29.cloned.1.call-start = ((), (), s32[]{:S(2)}) async-start(), calls=%async_computation.25 | async-start | bytes 2621440 | tf_op jit(solution)/shard_map/while/body/eval_jaxpr/reduce_scatter | solution.py:229
  1128.8 14.2 slice-start.2
  1131.3 11.6 slice-start
  1191.4 23.4 %copy-start.3 = (f32[256,1024]{1,0:T(8,128)S(1)}, f32[256,1024]{1,0:T(8,128)}, u32[]{:S(2)}) copy-start(f32[256,1024]{1,0:T(8,128)} %copy-done.2) | copy-start | bytes 3145732 | tf_op jit(solution)/shard_map/while
  1191.4 23.4 %copy-start.38 = (f32[256]{0:T(256)S(1)}, f32[256]{0:T(256)}, u32[]{:S(2)}) copy-start(f32[256]{0:T(256)} %copy-done.37) | copy-start | bytes 3076 | tf_op jit(solution)/shard_map/while
  1191.4 25.6 %copy-start.28 = (f32[1024]{0:T(1024)S(1)}, f32[1024]{0:T(1024)}, u32[]{:S(2)}) copy-start(f32[1024]{0:T(1024)} %copy-done.27) | copy-start | bytes 12292 | tf_op jit(solution)/shard_map/while
  1191.4 25.5 %copy-start.40 = (f32[1024]{0:T(1024)S(1)}, f32[1024]{0:T(1024)}, u32[]{:S(2)}) copy-start(f32[1024]{0:T(1024)} %copy-done.39) | copy-start | bytes 12292 | tf_op jit(solution)/shard_map/while
  1191.4 25.5 %copy-start.73 = (f32[1024]{0:T(1024)S(1)}, f32[1024]{0:T(1024)}, u32[]{:S(2)}) copy-start(f32[1024]{0:T(1024)} %copy-done.72) | copy-start | bytes 12292 | tf_op jit(solution)/shard_map/while
  1219.1 60.9 %reduce-scatter.17.cloned.1.call-start = ((), (), s32[]{:S(2)}) async-start(), calls=%async_computation.14 | async-start | bytes 1179648 | tf_op jit(solution)/shard_map/reduce_scatter | solution.py:284
  1219.7 78.9 %reduce-scatter.15.cloned.1.call-start = ((), (), s32[]{:S(2)}) async-start(), calls=%async_computation.13 | async-start | bytes 1179648 | tf_op jit(solution)/shard_map/reduce_scatter | solution.py:278
  1223.5 114.7 %reduce-scatter.11.cloned.1.call-start = ((), (), s32[]{:S(2)}) async-start(), calls=%async_computation.11 | async-start | bytes 1179648 | tf_op jit(solution)/shard_map/reduce_scatter | solution.py:274
  1224.1 153.9 %reduce-scatter.13.cloned.1.call-start = ((), (), s32[]{:S(2)}) async-start(), calls=%async_computation.12 | async-start | bytes 1179648 | tf_op jit(solution)/shard_map/reduce_scatter | solution.py:275
  1224.8 208.3 %reduce-scatter.19.cloned.1.call-start = ((), (), s32[]{:S(2)}) async-start(), calls=%async_computation.15 | async-start | bytes 4718592 | tf_op jit(solution)/shard_map/reduce_scatter | solution.py:281
  1224.9 15.5 %copy-start.47 = (f32[1024]{0:T(1024)S(1)}, f32[1024]{0:T(1024)}, u32[]{:S(2)}) copy-start(f32[1024]{0:T(1024)} %get-tuple-element.222) | copy-start | bytes 12292
  1224.9 15.5 %copy-start.50 = (f32[1024]{0:T(1024)S(1)}, f32[1024]{0:T(1024)}, u32[]{:S(2)}) copy-start(f32[1024]{0:T(1024)} %get-tuple-element.221) | copy-start | bytes 12292
  1224.9 15.5 %copy-start.53 = (f32[1024]{0:T(1024)S(1)}, f32[1024]{0:T(1024)}, u32[]{:S(2)}) copy-start(f32[1024]{0:T(1024)} %get-tuple-element.220) | copy-start | bytes 12292
  1224.9 15.5 %copy-start.56 = (f32[1024]{0:T(1024)S(1)}, f32[1024]{0:T(1024)}, u32[]{:S(2)}) copy-start(f32[1024]{0:T(1024)} %get-tuple-element.216) | copy-start | bytes 12292
  1224.9 15.5 %copy-start.59 = (f32[1024]{0:T(1024)S(1)}, f32[1024]{0:T(1024)}, u32[]{:S(2)}) copy-start(f32[1024]{0:T(1024)} %get-tuple-element.215) | copy-start | bytes 12292
  1224.9 15.5 %copy-start.62 = (f32[1024]{0:T(1024)S(1)}, f32[1024]{0:T(1024)}, u32[]{:S(2)}) copy-start(f32[1024]{0:T(1024)} %get-tuple-element.214) | copy-start | bytes 12292
  1225.6 263.1 %reduce-scatter.21.cloned.1.call-start = ((), (), s32[]{:S(2)}) async-start(), calls=%async_computation.16 | async-start | bytes 4718592 | tf_op jit(solution)/shard_map/reduce_scatter | solution.py:285
  (123 other events, 655.8 us)
Sparse Core Ops, SparseCore 0:
  19.6 48.6 all-gather.9
  88.6 75.4 reduce-scatter.22
  333.8 46.3 all-gather.17
  395.1 75.4 reduce-scatter.26
  621.5 45.1 all-gather.9
  687.0 75.4 reduce-scatter.22
  932.1 46.3 all-gather.17
  993.5 75.4 reduce-scatter.26
Sparse Core Ops, SparseCore 1:
  91.0 26.4 all-gather.13
  167.0 46.0 all-gather.11
  215.0 26.8 all-gather.15
  248.7 76.7 reduce-scatter.24
  573.9 42.2 reduce-scatter.28
  689.7 26.4 all-gather.13
  765.4 46.1 all-gather.11
  813.4 26.8 all-gather.15
  847.0 76.7 reduce-scatter.24
  1172.5 42.2 reduce-scatter.28
  1223.3 35.5 reduce-scatter.16
  1262.7 35.9 reduce-scatter.14
  1302.2 35.9 reduce-scatter.10
  1342.0 35.9 reduce-scatter.12
  1381.9 51.2 reduce-scatter.18
  1437.5 51.1 reduce-scatter.20
